TPU v7x, 512 devices: a whole 4x4x16 slice. The times are simulated.
512 devices in a mesh: seq: 32 (over z, core), heads: 4 (over x), dp: 4 (over y).
Axes of the slice: x: 4, y: 4, z: 16, core: 2. Of those that a mesh axis runs over, the one named last changes fastest.
Arguments:
- tokens: bfloat16 [4, 4096, 3072], P('dp', 'seq'), may hold values from -6 to 6
- proj_weights: bfloat16 [3, 3072, 4096], P(None, 'seq', ('heads', 'dp')), may hold values from -0.109375 to 0.109375
- norm_gain: float32 [4096], P(('heads', 'dp')), may hold values from 0.5 to 1.5
Outputs:
- attended: bfloat16 [4, 4096, 4096], P('dp', 'seq', 'heads')
All inputs are finite; a program needn't handle non-finite values.
Results may differ from a plain program's by a relative error of at most 0.0063.
Values may be sent and summed in bfloat16 or wider, within the bound.
No kernel may reach another device: no remote copies, remote signals or barrier semaphores. Data moves between devices by JAX's collectives and lax.ppermute only.
A program may use at most 64 MiB of HBM per device.

v0:
```python
import jax
import jax.numpy as jnp
from jax import lax
from jax.sharding import PartitionSpec as P

DH = 128


def prefix_2(part, axis, combine, identity):
    place = lax.axis_index(axis)
    gathered = lax.all_gather(part, axis)
    state = jnp.zeros_like(part) + jnp.asarray(identity, part.dtype)

    def one(step, state):
        return combine(state, lax.dynamic_index_in_dim(gathered, step, 0, False))

    return lax.fori_loop(0, place, one, state)


def add_pair(earlier, later):
    return earlier + later


def project_rows(flat_rows):

    def accumulate(total, piece, start):
        return jnp.einsum("nd,jdc->jnc", flat_rows, piece, preferred_element_type=jnp.float32)

    return accumulate


def to_heads(matrix, seq_count, length):
    return matrix.reshape(seq_count, length, -1, DH)


def activate(matrix, seq_count, length):
    return to_heads(jax.nn.silu(matrix).astype(jnp.bfloat16), seq_count, length)


def block_prefix(keys_b, values_b):
    state = jnp.einsum("sthd,sthe->shde", keys_b, values_b, preferred_element_type=jnp.float32)
    return prefix_2(state, "seq", add_pair, jnp.zeros_like(state))


def attend(queries, keys_b, values_b, prefix, norm_gain):
    seq_count, length, head_count, head_size = queries.shape
    scores = jnp.einsum("sthd,suhd->shtu", queries, keys_b, preferred_element_type=jnp.float32)
    causal = lax.broadcasted_iota(jnp.int32, (length, length), 0) >= lax.broadcasted_iota(
        jnp.int32, (length, length), 1
    )
    scores_b = jnp.where(causal, scores, 0.0).astype(jnp.bfloat16)
    local = jnp.einsum("shtu,suhd->sthd", scores_b, values_b, preferred_element_type=jnp.float32)
    carried = jnp.einsum(
        "sthd,shde->sthe", queries, prefix.astype(jnp.bfloat16), preferred_element_type=jnp.float32
    )
    attn = local + carried
    scale = lax.rsqrt(jnp.mean(attn * attn, axis=-1, keepdims=True) + 1e-06)
    normed = attn * scale * norm_gain.reshape(head_count, head_size)
    return normed.astype(jnp.bfloat16).reshape(seq_count, length, head_count * head_size)


def body(tokens, proj_weights, norm_gain):
    everyone = lax.all_gather(tokens, "dp", axis=0, tiled=True)
    seq_count, length, width = everyone.shape
    total_rows = seq_count * length
    per_device = proj_weights.shape[2]
    accumulate = project_rows(everyone.reshape(total_rows, width))
    start_sum = jnp.zeros((3, total_rows, per_device), jnp.float32)
    projected = accumulate(
        start_sum, lax.all_gather(proj_weights, "seq", axis=1, tiled=True), jnp.int32(0)
    )
    queries = activate(projected[0], seq_count, length)
    keys_b = activate(projected[1], seq_count, length)
    values_b = to_heads(projected[2].astype(jnp.bfloat16), seq_count, length)
    prefix = block_prefix(keys_b, values_b)
    normed = attend(queries, keys_b, values_b, prefix, norm_gain)
    return lax.all_to_all(normed, "dp", split_axis=0, concat_axis=2, tiled=True)


def solution(mesh):
    in_specs = (P("dp", "seq", None), P(None, "seq", ("heads", "dp")), P(("heads", "dp")))
    out_specs = P("dp", "seq", "heads")
    return jax.shard_map(body, mesh=mesh, in_specs=in_specs, out_specs=out_specs, check_vma=False)
```

profile of v0, /device:TPU:481, one launch (start us, length us, event | category | flops | bytes accessed | tf_op | source)
XLA Modules:
  0.0 297.7 jit_solution(694654217346947341)
XLA Ops:
  6.5 0.7 all-gather.7.cloned.1.call-update
  7.3 0.7 all-gather.5.cloned.1.call-update
  8.1 47.7 %all-gather.7.cloned.1.call-done = bf16[4,128,3072]{2,1,0:T(8,128)(2,1)} async-done(((bf16[1,128,3072]{2,1,0:T(8,128)(2,1)}), bf16[4,128,3072]{2,1,0:T(8,128)(2,1)}) %all-gather.7.cloned.1.call-update) | async-done | bytes 3145744 | tf_op jit(solution)/shard_map/all_gather | solution.py:63
  55.8 76.4 %all-gather.5.cloned.1.call-done = bf16[3,3072,256]{2,1,0:T(8,128)(2,1)} async-done(((bf16[3,96,256]{2,1,0:T(8,128)(2,1)}), bf16[3,3072,256]{2,1,0:T(8,128)(2,1)}) %all-gather.5.cloned.1.call-update) | async-done | bytes 4718608 | tf_op jit(solution)/shard_map/all_gather | solution.py:70
  132.1 5.5 %convolution_bitcast_fusion = f32[3,512,256]{1,2,0:T(8,128)S(1)} fusion(bf16[3,3072,256]{2,1,0:T(8,128)(2,1)} %all-gather.5.cloned.1.call-done, bf16[512,3072,1]{1,0,2:T(8,128)(2,1)} %bitcast.33), kind=kOutput, calls=%fused_computation.1 | convolution fusion | flops 2415919104 | bytes 9437184 | tf_op jit(solution)/shard_map/nd,jdc->jnc/dot_general | solution.py:27
  137.7 0.2 squeeze.12
  137.9 0.2 copy.16
  138.2 0.2 copy.19
  138.4 1.1 fusion.7
  139.6 0.2 squeeze.11
  139.8 0.2 copy.14
  140.0 0.6 fusion.2
  140.6 101.5 %all-gather.9.cloned.1.call-done = f32[128,2,128,128]{3,2,1,0:T(8,128)} async-done(((f32[4,2,128,128]{3,2,1,0:T(8,128)}), f32[128,2,128,128]{3,2,1,0:T(8,128)}) %all-gather.9.cloned.1.call-update) | async-done | bytes 16777232 | tf_op jit(solution)/shard_map/all_gather | solution.py:11
  242.2 37.0 %while.10 = (s32[]{:T(128)}, f32[4,2,128,128]{3,2,1,0:T(8,128)S(1)}, s32[]{:T(128)}, f32[32,4,2,128,128]{4,3,2,1,0:T(8,128)}, s32[]{:T(128)}, /*index=5*/s32[]{:T(128)}, s32[]{:T(128)}) while((s32[]{:T(128)}, f32[4,2,128,128]{3,2,1,0:T(8,128)S(1)}, s32[]{:T(128)}, f32[32,4,2,128,128]{4,3,2,1,0:T(8,128)}, s32[]{:T(128)}, /*index=5*/s32[]{:T(128)}, ...), condition=%wide.region_1.2_spmd, body=%wide.region_0.1_spmd.sunk | while | flops 131077 | bytes 1572987 | solution.py:17
  242.2 1.2 bitcast_add_fusion.2
  243.4 1.2 bitcast_add_fusion.2
  244.6 1.2 bitcast_add_fusion.2
  245.8 1.2 bitcast_add_fusion.2
  247.0 1.2 bitcast_add_fusion.2
  248.2 1.2 bitcast_add_fusion.2
  249.3 1.2 bitcast_add_fusion.2
  250.5 1.2 bitcast_add_fusion.2
  251.7 1.2 bitcast_add_fusion.2
  252.9 1.2 bitcast_add_fusion.2
  254.1 1.2 bitcast_add_fusion.2
  255.3 1.2 bitcast_add_fusion.2
  256.5 1.2 bitcast_add_fusion.2
  257.7 1.2 bitcast_add_fusion.2
  258.9 1.2 bitcast_add_fusion.2
  260.1 1.2 bitcast_add_fusion.2
  261.3 1.2 bitcast_add_fusion.2
  262.5 1.2 bitcast_add_fusion.2
  263.7 1.2 bitcast_add_fusion.2
  264.9 1.2 bitcast_add_fusion.2
  266.0 1.2 bitcast_add_fusion.2
  267.2 1.2 bitcast_add_fusion.2
  268.4 1.2 bitcast_add_fusion.2
  269.6 1.2 bitcast_add_fusion.2
  270.8 1.2 bitcast_add_fusion.2
  272.0 1.2 bitcast_add_fusion.2
  273.2 1.2 bitcast_add_fusion.2
  274.4 1.2 bitcast_add_fusion.2
  275.6 1.2 bitcast_add_fusion.2
  276.8 1.2 bitcast_add_fusion.2
  278.0 1.2 bitcast_add_fusion.2
  279.2 0.4 multiply_reduce_fusion
  279.7 10.6 %all_to_all.18 = bf16[4,128,256]{1,2,0:T(8,128)(2,1)S(1)} all-to-all(bf16[4,128,256]{1,2,0:T(8,128)(2,1)S(1)} %bitcast.29), channel_id=1, replica_groups=mesh['seq'=32,'heads'=4,'dp'=4] {'dp'}, dimensions={0} | all-to-all | bytes 524288 | tf_op jit(solution)/shard_map/all_to_all | solution.py:77
  290.3 0.8 copy.24
  (13 shorter events, 0.4 us)
Async XLA Ops:
  6.5 49.2 %all-gather.7.cloned.1.call-start = ((), (), s32[]{:S(2)}) async-start(), calls=%async_computation.2 | async-start | bytes 3932160 | tf_op jit(solution)/shard_map/all_gather | solution.py:63
  7.3 124.9 %all-gather.5.cloned.1.call-start = ((), (), s32[]{:S(2)}) async-start(), calls=%async_computation.1 | async-start | bytes 4866048 | tf_op jit(solution)/shard_map/all_gather | solution.py:70
  8.0 234.1 %all-gather.9.cloned.1.call-start = ((), (), s32[]{:S(2)}) async-start(), calls=%async_computation.3 | async-start | bytes 17301504 | tf_op jit(solution)/shard_map/all_gather | solution.py:11
  242.1 37.4 %copy-start = (f32[256]{0:T(256)S(1)}, f32[256]{0:T(256)}, u32[]{:S(2)}) copy-start(f32[256]{0:T(256)} %param.7) | copy-start | bytes 3076
Sparse Core Ops, SparseCore 0:
  9.5 46.2 all-gather.6
  57.9 74.1 all-gather.4
  139.7 102.3 all-gather.8
where the time goes:
time: 299 us; the launch traced here: 298 us
  waiting for transfers between devices  227 us (76%)
  other arithmetic  36.4 us (12%)
  between operations  13.2 us (4%)
  blocking collectives  10.6 us (4%)
  matrix products  7.57 us (3%)
    all_gather x1, waiting for transfers between devices, prefix_2(): gathered = lax.all_gather(part, axis)  101 us
    all_gather x1, waiting for transfers between devices, body(): lax.all_gather(proj_weights, 'seq', axis=1, tiled=True)  76.4 us
    all_gather x1, waiting for transfers between devices, body(): everyone = lax.all_gather(tokens, 'dp', axis=0, tiled=True)  47.7 us
    add x31, other arithmetic, add_pair(): return earlier + later  36.3 us
    all_to_all x1, blocking collectives, body(): return lax.all_to_all(normed, 'dp', split_axis=0, concat_axis=2, tiled=True)  10.6 us
  transfers between devices with their start and end apart: 3, of which 3 were waited for; matrix products, arithmetic and copies ran while one was open for 0% of the time, Pallas kernels for 0%

commit v1 on v0

--- a/solution.py
+++ b/solution.py
@@ -74,7 +74,10 @@
     values_b = to_heads(projected[2].astype(jnp.bfloat16), seq_count, length)
     prefix = block_prefix(keys_b, values_b)
     normed = attend(queries, keys_b, values_b, prefix, norm_gain)
-    return lax.all_to_all(normed, "dp", split_axis=0, concat_axis=2, tiled=True)
+    return jnp.concatenate(
+        lax.all_to_all(jnp.stack(jnp.split(normed, lax.axis_size("dp"), axis=0)), "dp", 0, 0),
+        axis=2,
+    )
 
 
 def solution(mesh):

time: 299 us -> 299 us (level)
  no operation moved by 1% of the time
where the time goes in v1:
time: 299 us; the launch traced here: 298 us
  waiting for transfers between devices  227 us (76%)
  other arithmetic  36.5 us (12%)
  between operations  13.2 us (4%)
  blocking collectives  10.6 us (4%)
  matrix products  7.56 us (3%)
    all_gather x1, waiting for transfers between devices, prefix_2(): gathered = lax.all_gather(part, axis)  101 us
    all_gather x1, waiting for transfers between devices, body(): lax.all_gather(proj_weights, 'seq', axis=1, tiled=True)  76.4 us
    all_gather x1, waiting for transfers between devices, body(): everyone = lax.all_gather(tokens, 'dp', axis=0, tiled=True)  47.7 us
    add x31, other arithmetic, add_pair(): return earlier + later  36.3 us
    all_to_all x1, blocking collectives, body(): lax.all_to_all(jnp.stack(jnp.split(normed, lax.axis_size('dp'), axis=0)),...  10.6 us
  transfers between devices with their start and end apart: 3, of which 3 were waited for; matrix products, arithmetic and copies ran while one was open for 0% of the time, Pallas kernels for 0%

profile of v1, /device:TPU:481, one launch (start us, length us, event | category | flops | bytes accessed | tf_op | source)
XLA Modules:
  0.0 297.8 jit_solution(12598075998898996331)
XLA Ops:
  6.5 0.7 all-gather.7.cloned.1.call-update
  7.3 0.7 all-gather.5.cloned.1.call-update
  8.1 47.7 %all-gather.7.cloned.1.call-done = bf16[4,128,3072]{2,1,0:T(8,128)(2,1)} async-done(((bf16[1,128,3072]{2,1,0:T(8,128)(2,1)}), bf16[4,128,3072]{2,1,0:T(8,128)(2,1)}) %all-gather.7.cloned.1.call-update) | async-done | bytes 3145744 | tf_op jit(solution)/shard_map/all_gather | solution.py:63
  55.8 76.4 %all-gather.5.cloned.1.call-done = bf16[3,3072,256]{2,1,0:T(8,128)(2,1)} async-done(((bf16[3,96,256]{2,1,0:T(8,128)(2,1)}), bf16[3,3072,256]{2,1,0:T(8,128)(2,1)}) %all-gather.5.cloned.1.call-update) | async-done | bytes 4718608 | tf_op jit(solution)/shard_map/all_gather | solution.py:70
  132.1 5.5 %convolution_bitcast_fusion = f32[3,512,256]{1,2,0:T(8,128)S(1)} fusion(bf16[3,3072,256]{2,1,0:T(8,128)(2,1)} %all-gather.5.cloned.1.call-done, bf16[512,3072,1]{1,0,2:T(8,128)(2,1)} %bitcast.37), kind=kOutput, calls=%fused_computation.1 | convolution fusion | flops 2415919104 | bytes 9437184 | tf_op jit(solution)/shard_map/nd,jdc->jnc/dot_general | solution.py:27
  137.7 0.2 squeeze.12
  137.9 0.2 copy.16
  138.2 0.2 copy.19
  138.4 1.1 fusion.7
  139.6 0.2 squeeze.11
  139.8 0.2 copy.14
  140.0 0.6 fusion.2
  140.6 101.5 %all-gather.9.cloned.1.call-done = f32[128,2,128,128]{3,2,1,0:T(8,128)} async-done(((f32[4,2,128,128]{3,2,1,0:T(8,128)}), f32[128,2,128,128]{3,2,1,0:T(8,128)}) %all-gather.9.cloned.1.call-update) | async-done | bytes 16777232 | tf_op jit(solution)/shard_map/all_gather | solution.py:11
  242.2 37.0 %while.10 = (s32[]{:T(128)}, f32[4,2,128,128]{3,2,1,0:T(8,128)S(1)}, s32[]{:T(128)}, f32[32,4,2,128,128]{4,3,2,1,0:T(8,128)}, s32[]{:T(128)}, /*index=5*/s32[]{:T(128)}, s32[]{:T(128)}) while((s32[]{:T(128)}, f32[4,2,128,128]{3,2,1,0:T(8,128)S(1)}, s32[]{:T(128)}, f32[32,4,2,128,128]{4,3,2,1,0:T(8,128)}, s32[]{:T(128)}, /*index=5*/s32[]{:T(128)}, ...), condition=%wide.region_1.2_spmd, body=%wide.region_0.1_spmd.sunk | while | flops 131077 | bytes 1572987 | solution.py:17
  242.2 1.2 bitcast_add_fusion.2
  243.4 1.2 bitcast_add_fusion.2
  244.6 1.2 bitcast_add_fusion.2
  245.8 1.2 bitcast_add_fusion.2
  247.0 1.2 bitcast_add_fusion.2
  248.1 1.2 bitcast_add_fusion.2
  249.3 1.2 bitcast_add_fusion.2
  250.5 1.2 bitcast_add_fusion.2
  251.7 1.2 bitcast_add_fusion.2
  252.9 1.2 bitcast_add_fusion.2
  254.1 1.2 bitcast_add_fusion.2
  255.3 1.2 bitcast_add_fusion.2
  256.5 1.2 bitcast_add_fusion.2
  257.7 1.2 bitcast_add_fusion.2
  258.9 1.2 bitcast_add_fusion.2
  260.1 1.2 bitcast_add_fusion.2
  261.3 1.2 bitcast_add_fusion.2
  262.5 1.2 bitcast_add_fusion.2
  263.7 1.2 bitcast_add_fusion.2
  264.9 1.2 bitcast_add_fusion.2
  266.0 1.2 bitcast_add_fusion.2
  267.2 1.2 bitcast_add_fusion.2
  268.4 1.2 bitcast_add_fusion.2
  269.6 1.2 bitcast_add_fusion.2
  270.8 1.2 bitcast_add_fusion.2
  272.0 1.2 bitcast_add_fusion.2
  273.2 1.2 bitcast_add_fusion.2
  274.4 1.2 bitcast_add_fusion.2
  275.6 1.2 bitcast_add_fusion.2
  276.8 1.2 bitcast_add_fusion.2
  278.0 1.2 bitcast_add_fusion.2
  279.2 0.4 multiply_reduce_fusion
  279.7 10.6 %all_to_all.5 = bf16[4,1,128,256]{2,3,1,0:T(8,128)(2,1)S(1)} all-to-all(bf16[4,1,128,256]{2,3,1,0:T(8,128)(2,1)S(1)} %pad_maximum_fusion), channel_id=1, replica_groups=mesh['seq'=32,'heads'=4,'dp'=4] {'dp'}, dimensions={0} | all-to-all | bytes 524288 | tf_op jit(solution)/shard_map/all_to_all | solution.py:78
  290.4 0.8 copy.24
  (15 shorter events, 0.5 us)
Async XLA Ops:
  6.5 49.2 %all-gather.7.cloned.1.call-start = ((), (), s32[]{:S(2)}) async-start(), calls=%async_computation.2 | async-start | bytes 3932160 | tf_op jit(solution)/shard_map/all_gather | solution.py:63
  7.3 124.9 %all-gather.5.cloned.1.call-start = ((), (), s32[]{:S(2)}) async-start(), calls=%async_computation.1 | async-start | bytes 4866048 | tf_op jit(solution)/shard_map/all_gather | solution.py:70
  8.0 234.1 %all-gather.9.cloned.1.call-start = ((), (), s32[]{:S(2)}) async-start(), calls=%async_computation.3 | async-start | bytes 17301504 | tf_op jit(solution)/shard_map/all_gather | solution.py:11
  242.1 37.4 %copy-start = (f32[256]{0:T(256)S(1)}, f32[256]{0:T(256)}, u32[]{:S(2)}) copy-start(f32[256]{0:T(256)} %param.7) | copy-start | bytes 3076
Sparse Core Ops, SparseCore 0:
  9.5 46.2 all-gather.6
  57.9 74.1 all-gather.4
  139.7 102.3 all-gather.8
